TPU v7x, 256 devices: a whole 4x4x8 slice. The times are simulated.
256 devices in a mesh: blk: 32 (over x, z), leaf: 4 (over y), samp: 2 (over core).
Axes of the slice: x: 4, y: 4, z: 8, core: 2. Of those that a mesh axis runs over, the one named last changes fastest.
Arguments:
- points: float32 [3, 32768], P(None, ('blk', 'leaf')), may hold values from 0 to 64, as said below
- neighbors: int32 [128, 8], P(('blk', 'leaf')), may hold values from -1 to 127, as said below
- omega: float32 [512, 32768], P(None, ('blk', 'leaf')), may hold values from -6 to 6
- observed: float32 [32768], P(('blk', 'leaf')), may hold values from -6 to 6
- prior_draws: float32 [64, 32768], P('samp', ('blk', 'leaf')), may hold values from -6 to 6
Outputs:
- weights: float32 [64, 32768], P('samp', ('blk', 'leaf'))
- residual: float32 [64, 32768], P('samp', ('blk', 'leaf'))
Inputs may be any that keep to these rules, and one draw needn't show every extreme that they name: Block g's points lie in the unit cell with integer corner (cx, cy, cz), where cx // 2 = g // 4 and 0 <= cy, cz < 3. `neighbors`: row g lists in ascending order every block h whose unit cell touches g's (cells at most one apart in every coordinate, the first taken periodic of period 2 * 32), which includes every block with a point within distance 1 of a point of g, followed by -1 in the unused slots; the relation is symmetric, and every listed block has a slab index h // 4 equal to or cyclically next to g // 4.
All inputs are finite; a program needn't handle non-finite values.
Results may differ from a plain program's by a relative error of at most 0.0003.
Values sent between devices are 32-bit elements; how exact they have to be, the bound alone decides.
A program may use at most 64 MiB of HBM per device.

v0:
```python
import jax
import jax.numpy as jnp
from jax import lax
from jax.sharding import PartitionSpec as P
from jax.experimental import pallas as pl
from jax.experimental.pallas import tpu as pltpu

PB = 256
ITERS = 2


support_radius = 0.8
noise_variance = 1.0
sketch_shift = 1.0

ALL_AXES = ("blk", "leaf", "samp")


def shifted_2(block, axis, distance):
    devices = range(lax.axis_size(axis))
    route = [((i - distance) % len(devices), i) for i in devices]
    return lax.ppermute(block, axis, route)


def wendland(row_points, column_points, period):
    offset = row_points[None, :, :, None] - column_points[:, :, None, :]
    half_period = 0.5 * period
    along_x = jnp.mod(offset[:, 0] + half_period, period) - half_period
    squared = along_x * along_x + offset[:, 1] * offset[:, 1] + offset[:, 2] * offset[:, 2]
    radius = jnp.sqrt(squared) / support_radius
    remain = jnp.maximum(1.0 - radius, 0.0)
    return remain**4 * (4.0 * radius + 1.0)


def high_dot(left, right):
    return jnp.dot(left, right, precision=lax.Precision.HIGHEST, preferred_element_type=jnp.float32)


def shifted(values, offset_by):
    return shifted_2(values, "blk", offset_by)


def beside_all(values):
    slab_values = lax.all_gather(values, "leaf", axis=1, tiled=True)
    return jnp.concatenate([shifted(slab_values, 1), slab_values, shifted(slab_values, -1)], axis=1)


def blk_split(n_blk):
    if n_blk % 8 == 0 and n_blk > 8:
        return (8, n_blk // 8)
    return (n_blk, 1)


def reduce_phases():
    inner, outer = blk_split(lax.axis_size("blk"))
    phases = [("leaf", lax.axis_size("leaf"), 1), ("blk", inner, 1)]
    if outer > 1:
        phases.append(("blk", outer, inner))
    return tuple(p for p in phases if p[1] > 1)


def group_peer(axis, n, stride, k):
    idx = lax.axis_index(axis)
    own = (idx // stride) % n
    return own, idx + ((own + k) % n - own) * stride


def sum_kernel(phases, x_ref, o_ref, recv, send_sem, recv_sem):
    barrier = pltpu.get_barrier_semaphore()
    greeted = 0
    for axis, n, stride in phases:
        for k in range(1, n):
            _, peer = group_peer(axis, n, stride, k)
            pl.semaphore_signal(
                barrier, 1, device_id={axis: peer}, device_id_type=pl.DeviceIdType.MESH
            )
            greeted += 1
    pl.semaphore_wait(barrier, greeted)
    acc = x_ref[...]
    for p, (axis, n, stride) in enumerate(phases):
        recv[p, 0] = acc
        copies = []
        for k in range(1, n):
            own, peer = group_peer(axis, n, stride, k)
            copy = pltpu.make_async_remote_copy(
                src_ref=x_ref if p == 0 else recv.at[p, 0],
                dst_ref=recv.at[p, k],
                send_sem=send_sem.at[p, k],
                recv_sem=recv_sem.at[p, k],
                device_id={axis: peer},
                device_id_type=pl.DeviceIdType.MESH,
            )
            copy.start()
            copies.append(copy)
        for copy in copies:
            copy.wait()
        own, _ = group_peer(axis, n, stride, 0)
        terms = [recv[p, (own - j) % n] for j in range(n)]
        acc = terms[0]
        for term in terms[1:]:
            acc = acc + term
    o_ref[...] = acc


def group_sum(values, collective_id):
    phases = reduce_phases()
    rows = values.shape[0]
    widest = max(n for _, n, _ in phases)
    return pl.pallas_call(
        lambda *refs: sum_kernel(phases, *refs),
        out_shape=jax.ShapeDtypeStruct(values.shape, jnp.float32),
        in_specs=[pl.BlockSpec(memory_space=pltpu.VMEM)],
        out_specs=pl.BlockSpec(memory_space=pltpu.VMEM),
        scratch_shapes=[
            pltpu.VMEM((len(phases), widest, rows, 128), jnp.float32),
            pltpu.SemaphoreType.DMA((len(phases), widest)),
            pltpu.SemaphoreType.DMA((len(phases), widest)),
        ],
        compiler_params=pltpu.CompilerParams(collective_id=collective_id, has_side_effects=True),
    )(values)


def gram_kernel(phases, x_ref, y_ref, o_ref, z_ref, *scratch):
    count = len(phases)
    recvs = scratch[: count - 1]
    sums = scratch[count - 1 : 2 * count - 3]
    full = scratch[2 * count - 3]
    rs_send, rs_recv, ag_send, ag_recv, side, side_send, side_recv = scratch[2 * count - 2 :]
    side_acc = y_ref[...]
    outer_own, _ = group_peer(*phases[0], 0)
    barrier = pltpu.get_barrier_semaphore()
    greeted = 0
    for axis, n, stride in phases:
        for k in range(1, n):
            _, peer = group_peer(axis, n, stride, k)
            pl.semaphore_signal(
                barrier, 1, device_id={axis: peer}, device_id_type=pl.DeviceIdType.MESH
            )
            greeted += 1
    pl.semaphore_wait(barrier, greeted)
    source = x_ref
    length = x_ref.shape[0]
    offset = outer_own * length
    for p, (axis, n, stride) in enumerate(phases):
        if p == 0:
            continue
        own, _ = group_peer(axis, n, stride, 0)
        part = length // n
        recv = recvs[p - 1]
        recv[0] = source[pl.ds(pl.multiple_of(own * part, 8), part)]
        copies = []
        if axis != "samp":
            side[p, 0] = side_acc
            for k in range(1, n):
                _, peer = group_peer(axis, n, stride, k)
                copy = pltpu.make_async_remote_copy(
                    src_ref=side.at[p, 0],
                    dst_ref=side.at[p, k],
                    send_sem=side_send.at[p, k],
                    recv_sem=side_recv.at[p, k],
                    device_id={axis: peer},
                    device_id_type=pl.DeviceIdType.MESH,
                )
                copy.start()
                copies.append(copy)
        for k in range(1, n):
            _, peer = group_peer(axis, n, stride, k)
            chunk = (own + k) % n
            copy = pltpu.make_async_remote_copy(
                src_ref=source.at[pl.ds(pl.multiple_of(chunk * part, 8), part)],
                dst_ref=recv.at[k],
                send_sem=rs_send.at[p, k],
                recv_sem=rs_recv.at[p, k],
                device_id={axis: peer},
                device_id_type=pl.DeviceIdType.MESH,
            )
            copy.start()
            copies.append(copy)
        for copy in copies:
            copy.wait()
        acc = recv[own % n]
        for j in range(1, n):
            acc = acc + recv[(own - j) % n]
        if axis != "samp":
            side_acc = side[p, own % n]
            for j in range(1, n):
                side_acc = side_acc + side[p, (own - j) % n]
        offset = offset + own * part
        length = part
        if p < count - 1:
            sums[p - 1][...] = acc
            source = sums[p - 1]
        else:
            full[pl.ds(pl.multiple_of(offset, 8), part)] = acc
    for p in reversed(range(count)):
        axis, n, stride = phases[p]
        own, _ = group_peer(axis, n, stride, 0)
        here = full.at[pl.ds(pl.multiple_of(offset, 8), length)]
        copies = []
        for k in range(1, n):
            _, peer = group_peer(axis, n, stride, k)
            copy = pltpu.make_async_remote_copy(
                src_ref=here,
                dst_ref=here,
                send_sem=ag_send.at[p, k],
                recv_sem=ag_recv.at[p, k],
                device_id={axis: peer},
                device_id_type=pl.DeviceIdType.MESH,
            )
            copy.start()
            copies.append(copy)
        for copy in copies:
            copy.wait()
        offset = offset - own * length
        length = length * n
    o_ref[...] = full[...]
    z_ref[...] = side_acc


def gram_sum(values, side_values, collective_id):
    phases = (("samp", lax.axis_size("samp"), 1),) + reduce_phases()
    rows = values.shape[0]
    widest = max(n for _, n, _ in phases)
    recvs, sums = [], []
    length = rows
    for p, (_, n, _) in enumerate(phases):
        if p == 0:
            continue
        length //= n
        recvs.append(pltpu.VMEM((n, length, 128), jnp.float32))
        if p < len(phases) - 1:
            sums.append(pltpu.VMEM((length, 128), jnp.float32))
    rows = rows * phases[0][1]
    semaphores = [pltpu.SemaphoreType.DMA((len(phases), widest)) for _ in range(4)]
    side_scratch = [
        pltpu.VMEM((len(phases), widest) + side_values.shape, jnp.float32),
        pltpu.SemaphoreType.DMA((len(phases), widest)),
        pltpu.SemaphoreType.DMA((len(phases), widest)),
    ]
    return pl.pallas_call(
        lambda *refs: gram_kernel(phases, *refs),
        out_shape=(
            jax.ShapeDtypeStruct((rows, 128), jnp.float32),
            jax.ShapeDtypeStruct(side_values.shape, jnp.float32),
        ),
        in_specs=[pl.BlockSpec(memory_space=pltpu.VMEM)] * 2,
        out_specs=(pl.BlockSpec(memory_space=pltpu.VMEM),) * 2,
        scratch_shapes=recvs + sums + [pltpu.VMEM((rows, 128), jnp.float32)] + semaphores + side_scratch,
        compiler_params=pltpu.CompilerParams(collective_id=collective_id, has_side_effects=True),
    )(values, side_values)


def halo_kernel(n_blk, n_leaf, wide, x_ref, o_ref, land, send_sem, recv_sem):
    own_blk = lax.axis_index("blk")
    own_leaf = lax.axis_index("leaf")
    centre = n_leaf if wide else 0
    targets = []
    for d in (-1, 1) if wide else ():
        for leaf in range(n_leaf):
            targets.append(((own_blk + d + n_blk) % n_blk, leaf, (1 - d) * n_leaf + own_leaf))
    for k in range(1, n_leaf):
        targets.append((own_blk, (own_leaf + k) % n_leaf, centre + own_leaf))
    barrier = pltpu.get_barrier_semaphore()
    for blk, leaf, _ in targets:
        pl.semaphore_signal(
            barrier,
            1,
            device_id={"blk": blk, "leaf": leaf},
            device_id_type=pl.DeviceIdType.MESH,
        )
    pl.semaphore_wait(barrier, len(targets))
    copies = []
    for i, (blk, leaf, segment) in enumerate(targets):
        copy = pltpu.make_async_remote_copy(
            src_ref=x_ref,
            dst_ref=land.at[segment],
            send_sem=send_sem.at[i],
            recv_sem=recv_sem.at[segment],
            device_id={"blk": blk, "leaf": leaf},
            device_id_type=pl.DeviceIdType.MESH,
        )
        copy.start()
        copies.append(copy)
    land[centre + own_leaf] = x_ref[...]
    incoming = []
    if wide:
        incoming += [((own_blk - 1 + n_blk) % n_blk, s, s) for s in range(n_leaf)]
        incoming += [((own_blk + 1) % n_blk, s, 2 * n_leaf + s) for s in range(n_leaf)]
    for k in range(1, n_leaf):
        leaf = (own_leaf + k) % n_leaf
        incoming.append((own_blk, leaf, centre + leaf))
    for copy in copies:
        copy.wait_send()
    for blk, leaf, segment in incoming:
        pltpu.make_async_remote_copy(
            src_ref=x_ref,
            dst_ref=land.at[segment],
            send_sem=send_sem.at[0],
            recv_sem=recv_sem.at[segment],
            device_id={"blk": blk, "leaf": leaf},
            device_id_type=pl.DeviceIdType.MESH,
        ).wait_recv()
    o_ref[...] = land[...]


def halo_gather(values, collective_id, wide=True):
    n_blk = lax.axis_size("blk")
    n_leaf = lax.axis_size("leaf")
    segments = (3 if wide else 1) * n_leaf
    return pl.pallas_call(
        lambda *refs: halo_kernel(n_blk, n_leaf, wide, *refs),
        out_shape=jax.ShapeDtypeStruct((segments,) + values.shape, jnp.float32),
        in_specs=[pl.BlockSpec(memory_space=pltpu.VMEM)],
        out_specs=pl.BlockSpec(memory_space=pltpu.VMEM),
        scratch_shapes=[
            pltpu.VMEM((segments,) + values.shape, jnp.float32),
            pltpu.SemaphoreType.DMA((segments,)),
            pltpu.SemaphoreType.DMA((segments,)),
        ],
        compiler_params=pltpu.CompilerParams(collective_id=collective_id, has_side_effects=True),
    )(values)


def blocked_factor(gram, block=128):
    count = gram.shape[0] // block
    eye = jnp.eye(block, dtype=jnp.float32)
    inverses, panels = [], []
    rest = gram
    for k in range(count):
        diagonal = lax.linalg.cholesky(rest[:block, :block])
        inverse = lax.linalg.triangular_solve(diagonal, eye, left_side=True, lower=True)
        inverses.append(inverse)
        if k < count - 1:
            panel = high_dot(rest[block:, :block], inverse.T)
            panels.append(panel)
            rest = rest[block:, block:] - high_dot(panel, panel.T)
    return inverses, panels


def blocked_solve(inverses, panels, values):
    block = inverses[0].shape[0]
    count = len(inverses)
    lower = []
    rest = values
    for k in range(count):
        part = high_dot(inverses[k], rest[:block])
        lower.append(part)
        if k < count - 1:
            rest = rest[block:] - high_dot(panels[k], part)
    upper = [None] * count
    for k in reversed(range(count)):
        rhs = lower[k]
        if k < count - 1:
            rhs = rhs - high_dot(panels[k].T, jnp.concatenate(upper[k + 1 :]))
        upper[k] = high_dot(inverses[k].T, rhs)
    return jnp.concatenate(upper)


def lower_solve(factor, values):
    return lax.linalg.triangular_solve(factor, values, left_side=True, lower=True)


def local(points, neighbors, omega, observed, prior_draws):
    blk_dev = neighbors.shape[0]
    cycle_count = lax.axis_size("blk")
    slab_blocks = blk_dev * lax.axis_size("leaf")
    period = 2.0 * cycle_count
    own_slab = lax.axis_index("blk")
    n_samp = lax.axis_size("samp")
    samp_idx = lax.axis_index("samp")
    usable = neighbors >= 0
    relative = jnp.mod(neighbors // slab_blocks - own_slab + 1, cycle_count)
    chosen = jnp.where(usable, relative * slab_blocks + jnp.mod(neighbors, slab_blocks), 0)
    usable_weight = usable.astype(jnp.float32)
    reach_blocks = halo_gather(points, 4)
    row_blocks = points.reshape(3, blk_dev, PB).transpose(1, 0, 2)

    segments = 3 * slab_blocks
    listed = jnp.zeros((segments,), jnp.float32).at[chosen[0]].max(usable_weight[0])
    kernel_tile = wendland(row_blocks[0], reach_blocks, period) * listed[:, None, None]

    def apply_kernel(values, wide=False):
        width = values.shape[0]
        if wide:
            slab_values = halo_gather(values, 5, wide=False)
            parts = (shifted(slab_values, 1), slab_values, shifted(slab_values, -1))
            out = None
            for i, part in enumerate(parts):
                tile = kernel_tile[i * slab_blocks : (i + 1) * slab_blocks]
                term = jnp.einsum("ncj,nij->ci", part, tile, precision=lax.Precision.HIGHEST)
                out = term if out is None else out + term
            return out
        reach = halo_gather(values, 6)
        return jnp.einsum("ncj,nij->ci", reach, kernel_tile, precision=lax.Precision.HIGHEST)

    def slot(x):
        zeros = jnp.zeros((n_samp,) + x.shape, x.dtype)
        return lax.dynamic_update_index_in_dim(zeros, x, samp_idx, 0)

    def unslot(xs):
        return lax.dynamic_index_in_dim(xs, samp_idx, 0, keepdims=False)

    def total_per_samp(values):
        return jax.tree.map(unslot, lax.psum(jax.tree.map(slot, values), ALL_AXES))

    sketch_rows = omega.shape[0]
    omega_rows = lax.dynamic_slice_in_dim(omega, samp_idx * (sketch_rows // n_samp), sketch_rows // n_samp)
    sketch_own = apply_kernel(omega_rows, wide=True) + sketch_shift * omega_rows
    sketch = lax.all_gather(sketch_own, "samp", axis=0, tiled=True)
    rhs = observed[None, :] - prior_draws
    joint_part = 0.5 * (high_dot(omega_rows, sketch.T) + high_dot(sketch_own, omega.T)) + high_dot(
        sketch_own, sketch.T
    )
    gram_rows = joint_part.shape[1]
    width = rhs.shape[0]
    rhs_proj = high_dot(sketch, rhs.T).reshape(gram_rows * width // 128, 128)
    joint_gram, rhs_proj = gram_sum(joint_part.reshape(-1, 128), rhs_proj, 2)
    joint_gram = joint_gram.reshape(gram_rows, gram_rows)
    rhs_proj = rhs_proj.reshape(gram_rows, width)

    inverses, panels = blocked_factor(joint_gram)

    def precond_from(vectors, projected):
        solved = blocked_solve(inverses, panels, projected)
        return (vectors - high_dot(solved.T, sketch)) / noise_variance, solved

    residual = rhs
    projected = rhs_proj
    precond, _ = precond_from(residual, projected)
    direction = precond
    weights = jnp.zeros_like(rhs)

    sketch_rows = sketch.shape[0]

    def pack_scalars(*vectors):
        rows = jnp.stack(vectors)
        return jnp.pad(rows, ((0, 8 - rows.shape[0]), (0, 128 - width)))

    image = apply_kernel(direction) + noise_variance * direction
    image_proj = high_dot(sketch, image.T).reshape(sketch_rows * width // 128, 128)
    packed = jnp.concatenate(
        [
            image_proj,
            pack_scalars(
                jnp.sum(residual * precond, axis=1),
                jnp.sum(direction * image, axis=1),
                jnp.sum(residual * residual, axis=1),
                jnp.sum(residual * image, axis=1),
                jnp.sum(image * image, axis=1),
            ),
        ]
    )
    packed = group_sum(packed, 0)
    image_proj = packed[:-8].reshape(sketch_rows, width)
    inner_now = packed[-8, :width]
    curvature = packed[-7, :width]
    residual_sq, residual_image, image_sq = packed[-6, :width], packed[-5, :width], packed[-4, :width]
    step_size = inner_now / curvature
    weights = weights + step_size[:, None] * direction
    residual = residual - step_size[:, None] * image
    projected = projected - step_size[None, :] * image_proj
    precond, solved = precond_from(residual, projected)
    residual_sq = residual_sq - 2.0 * step_size * residual_image + step_size * step_size * image_sq
    inner_next = (residual_sq - jnp.sum(projected * solved, axis=0)) / noise_variance
    direction = precond + (inner_next / inner_now)[:, None] * direction
    inner_now = inner_next

    image = apply_kernel(direction) + noise_variance * direction
    curvature = group_sum(pack_scalars(jnp.sum(direction * image, axis=1)), 1)[0, :width]
    step_size = inner_now / curvature
    weights = weights + step_size[:, None] * direction
    residual = residual - step_size[:, None] * image
    return (weights, residual)


def solution(mesh):
    in_specs = (
        P(None, ("blk", "leaf")),
        P(("blk", "leaf"), None),
        P(None, ("blk", "leaf")),
        P(("blk", "leaf")),
        P("samp", ("blk", "leaf")),
    )
    out_specs = (P("samp", ("blk", "leaf")), P("samp", ("blk", "leaf")))
    return jax.shard_map(local, mesh=mesh, in_specs=in_specs, out_specs=out_specs, check_vma=False)
```

profile of v0, /device:TPU:4, one launch (start us, length us, event | category | flops | bytes accessed | tf_op | source)
XLA Modules:
  0.0 331.2 jit_solution(8265518543682222377)
XLA Ops:
  0.6 1.0 copy-done
  2.4 18.2 %shard_map.68 = f32[4,256,256]{2,1,0:T(8,128)} custom-call(f32[256,256]{1,0:T(8,128)} %constant_dynamic-slice_fusion.refs_0_), custom_call_target="tpu_custom_call" | custom-call | tf_op jit(solution)/shard_map/pallas_call | solution.py:310
  20.6 5.9 %collective-permute-start.1 = (f32[4,256,256]{2,1,0:T(8,128)}, f32[4,256,256]{2,1,0:T(8,128)S(1)}, u32[]{:S(2)}, u32[]{:S(2)}) collective-permute-start(f32[4,256,256]{2,1,0:T(8,128)} %shard_map.68), channel_id=1, source_target_pairs={{8,0},{16,8},{24,16},{32,24},{40,32},{48,40},{56,48},{64,56},{72,6... | collective-permute-start | bytes 3145736 | tf_op jit(solution)/shard_map/ppermute | solution.py:22
  27.2 28.8 %shard_map.69 = f32[12,3,256]{2,1,0:T(4,128)} custom-call(f32[3,256]{1,0:T(4,128)} %refs_0_.1), custom_call_target="tpu_custom_call" | custom-call | tf_op jit(solution)/shard_map/pallas_call | solution.py:310
  56.0 0.8 copy.25
  56.8 5.5 %broadcast_subtract_fusion = f32[12,3,256,256]{3,2,0,1:T(8,128)} fusion(f32[12,3,256]{2,0,1:T(8,128)S(1)} %copy.25, f32[3,256]{1,0:T(4,128)} %refs_0_.1), kind=kLoop, calls=%fused_computation.2 | loop fusion | flops 2359296 | bytes 9477120 | tf_op jit(solution)/shard_map/sub | solution.py:26
  63.0 6.4 %multiply_multiply_fusion = f32[12,256,256]{2,1,0:T(8,128)S(1)} fusion(f32[12,3,256,256]{3,2,0,1:T(8,128)} %broadcast_subtract_fusion, f32[12]{0:T(128)S(1)} %scatter_custom_fusion), kind=kLoop, calls=%fused_computation.15 | loop fusion | flops 17301504 | bytes 12582960 | tf_op jit(solution)/shard_map/mul | solution.py:380
  69.4 1.0 convolution_bitcast_fusion.1
  70.5 1.0 convolution_bitcast_fusion
  71.5 1.0 fusion.12
  72.6 2.4 all_gather.3
  76.9 0.8 reshape.134.refs_0_
  79.0 56.9 %shard_map.70 = (f32[2048,128]{1,0:T(8,128)}, f32[128,128]{1,0:T(8,128)}) custom-call(f32[1024,128]{1,0:T(8,128)} %reshape.134.refs_0_, f32[128,128]{1,0:T(8,128)} %reshape.135.refs_1_), custom_call_target="tpu_custom_call" | custom-call | tf_op jit(solution)/shard_map/pallas_call | solution.py:240
  137.4 1.4 reshape.136
  139.0 11.7 %custom-call.12 = f32[128,128]{1,0:T(8,128)S(1)} custom-call(f32[128,128]{1,0:T(8,128)S(1)} %fusion.50), custom_call_target="Cholesky" | custom-call | tf_op jit(solution)/shard_map/cholesky/custom-call.1 | solution.py:330
  152.1 9.8 %custom-call.13 = f32[1,128,128]{1,2,0:T(8,128)S(1)} custom-call(f32[1,128,128]{2,1,0:T(8,128)S(1)} %fusion.31), custom_call_target="InvertDiagBlocksLowerTriangular" | custom-call | tf_op jit(solution)/shard_map/triangular_solve/custom-call.0 | solution.py:331
  164.2 11.9 %custom-call.14 = f32[128,128]{1,0:T(8,128)S(1)} custom-call(f32[128,128]{1,0:T(8,128)S(1)} %copy.33), custom_call_target="Cholesky" | custom-call | tf_op jit(solution)/shard_map/cholesky/custom-call.1 | solution.py:330
  177.5 9.8 %custom-call.15 = f32[1,128,128]{1,2,0:T(8,128)S(1)} custom-call(f32[1,128,128]{2,1,0:T(8,128)S(1)} %fusion.32), custom_call_target="InvertDiagBlocksLowerTriangular" | custom-call | tf_op jit(solution)/shard_map/triangular_solve/custom-call.0 | solution.py:331
  189.3 11.7 %custom-call.16 = f32[128,128]{1,0:T(8,128)S(1)} custom-call(f32[128,128]{1,0:T(8,128)S(1)} %fusion.46), custom_call_target="Cholesky" | custom-call | tf_op jit(solution)/shard_map/cholesky/custom-call.1 | solution.py:330
  202.4 10.2 %custom-call.17 = f32[1,128,128]{1,2,0:T(8,128)S(1)} custom-call(f32[1,128,128]{2,1,0:T(8,128)S(1)} %fusion.33), custom_call_target="InvertDiagBlocksLowerTriangular" | custom-call | tf_op jit(solution)/shard_map/triangular_solve/custom-call.0 | solution.py:331
  214.1 11.7 %custom-call.18 = f32[128,128]{1,0:T(8,128)S(1)} custom-call(f32[128,128]{1,0:T(8,128)S(1)} %broadcast_multiply_fusion), custom_call_target="Cholesky" | custom-call | tf_op jit(solution)/shard_map/cholesky/custom-call.1 | solution.py:330
  227.1 9.8 %custom-call.19 = f32[1,128,128]{1,2,0:T(8,128)S(1)} custom-call(f32[1,128,128]{2,1,0:T(8,128)S(1)} %fusion.34), custom_call_target="InvertDiagBlocksLowerTriangular" | custom-call | tf_op jit(solution)/shard_map/triangular_solve/custom-call.0 | solution.py:331
  238.9 1.0 convolution_subtract_fusion.8.refs_0_
  239.8 11.0 %shard_map.71 = f32[12,32,256]{2,1,0:T(8,128)} custom-call(f32[32,256]{1,0:T(8,128)} %convolution_subtract_fusion.8.refs_0_), custom_call_target="tpu_custom_call" | custom-call | tf_op jit(solution)/shard_map/pallas_call | solution.py:310
  250.9 5.0 %multiply_reduce_fusion.3 = (f32[32]{0:T(128)S(1)}, f32[32]{0:T(128)S(1)}, f32[32]{0:T(128)S(1)}, f32[32]{0:T(128)S(1)}, f32[32]{0:T(128)S(1)}, /*index=5*/f32[32,256]{1,0:T(8,128)S(1)}) fusion(f32[32,256]{1,0:T(8,128)S(1)} %copy-done.4, f32[256]{0:T(256)S(1)} %copy-done.8, f32[32,256]{1,0:T(8,128)} %convolution_subtract_fusion.8.refs_0_, ...), kind=kOutput, calls=%fused_computation.122 | convolution fusion | flops 302088032 | bytes 3638912 | tf_op jit(solution)/shard_map/ncj,nij->ci/dot_general | solution.py:394
  257.4 30.6 %shard_map.72 = f32[136,128]{1,0:T(8,128)} custom-call(f32[136,128]{1,0:T(8,128)} %select_maximum_fusion.refs_0_), custom_call_target="tpu_custom_call" | custom-call | tf_op jit(solution)/shard_map/pallas_call | solution.py:109
  287.9 0.8 slice.142
  293.3 0.9 bitcast_divide_fusion.2
  294.2 1.0 fusion.15.refs_0_
  295.2 10.3 %shard_map.73 = f32[12,32,256]{2,1,0:T(8,128)} custom-call(f32[32,256]{1,0:T(8,128)} %fusion.15.refs_0_), custom_call_target="tpu_custom_call" | custom-call | tf_op jit(solution)/shard_map/pallas_call | solution.py:310
  305.5 4.9 %multiply_reduce_fusion.1 = (f32[32]{0:T(128)S(1)}, f32[32,256]{1,0:T(8,128)S(1)}) fusion(f32[32,256]{1,0:T(8,128)} %fusion.15.refs_0_, f32[12,32,256]{2,1,0:T(8,128)} %shard_map.73, f32[12,256,256]{2,1,0:T(8,128)} %copy-done.1), kind=kOutput, calls=%fused_computation.119 | convolution fusion | flops 302014432 | bytes 3604608 | tf_op jit(solution)/shard_map/ncj,nij->ci/dot_general | solution.py:394
  311.0 18.6 %shard_map.74 = f32[8,128]{1,0:T(8,128)} custom-call(f32[8,128]{1,0:T(8,128)} %pad.9.refs_0_), custom_call_target="tpu_custom_call" | custom-call | tf_op jit(solution)/shard_map/pallas_call | solution.py:109
  (116 shorter events, 27.7 us)
Async XLA Ops:
  0.6 1.0 copy-start
  20.6 49.9 %collective-permute-start.1 = (f32[4,256,256]{2,1,0:T(8,128)}, f32[4,256,256]{2,1,0:T(8,128)S(1)}, u32[]{:S(2)}, u32[]{:S(2)}) collective-permute-start(f32[4,256,256]{2,1,0:T(8,128)} %shard_map.68), channel_id=1, source_target_pairs={{8,0},{16,8},{24,16},{32,24},{40,32},{48,40},{56,48},{64,56},{72,6... | collective-permute-start | bytes 3145736 | tf_op jit(solution)/shard_map/ppermute | solution.py:22
  26.5 45.0 %collective-permute-start = (f32[4,256,256]{2,1,0:T(8,128)}, f32[4,256,256]{2,1,0:T(8,128)S(1)}, u32[]{:S(2)}, u32[]{:S(2)}) collective-permute-start(f32[4,256,256]{2,1,0:T(8,128)} %shard_map.68), channel_id=1, source_target_pairs={{248,0},{0,8},{8,16},{16,24},{24,32},{32,40},{40,48},{48,56},{56,6... | collective-permute-start | bytes 3145736 | tf_op jit(solution)/shard_map/ppermute | solution.py:22
  56.8 5.5 %copy-start.9 = (s32[1,8]{1,0:T(1,128)S(1)}, s32[1,8]{1,0:T(1,128)}, u32[]{:S(2)}) copy-start(s32[1,8]{1,0:T(1,128)} %param.9) | copy-start | bytes 100
  62.9 6.4 %copy-start.3 = (f32[4,256,256]{2,1,0:T(8,128)S(1)}, f32[4,256,256]{2,1,0:T(8,128)}, u32[]{:S(2)}) copy-start(f32[4,256,256]{2,1,0:T(8,128)} %shard_map.68) | copy-start | bytes 3145732
  69.4 3.2 copy-start.1
  69.4 2.1 copy-start.2
  74.9 2.8 copy-start.4
  74.9 2.8 copy-start.8
  238.8 50.7 %copy-start.7 = (f32[128,128]{1,0:T(8,128)S(1)}, f32[128,128]{1,0:T(8,128)}, u32[]{:S(2)}) copy-start(f32[128,128]{1,0:T(8,128)} %get-tuple-element.7) | copy-start | bytes 196612
  255.8 38.4 %copy-start.5 = (f32[32,256]{1,0:T(8,128)S(1)}, f32[32,256]{1,0:T(8,128)}, u32[]{:S(2)}) copy-start(f32[32,256]{1,0:T(8,128)} %convolution_subtract_fusion.8.refs_0_) | copy-start | bytes 98308
  295.2 35.2 %copy-start.6 = (f32[32,256]{1,0:T(8,128)S(1)}, f32[32,256]{1,0:T(8,128)}, u32[]{:S(2)}) copy-start(f32[32,256]{1,0:T(8,128)} %fusion.15.refs_0_) | copy-start | bytes 98308
where the time goes:
time: 338 us; the launch traced here: 331 us
  Pallas kernels  174 us (51%)
  other arithmetic  109 us (32%)
  matrix products  27.5 us (8%)
  local copies, waits for them, and re-layouts  10.3 us (3%)
  starting transfers between devices  5.91 us (2%)
    pallas_call x4, Pallas kernels, halo_gather(): pl.pallas_call(lambda *refs: halo_kernel(n_blk, n_leaf, wide, *refs), out...  68.3 us
    pallas_call x1, Pallas kernels, gram_sum(): pl.pallas_call(lambda *refs: gram_kernel(phases, *refs), out_shape=(jax.S...  56.9 us
    another operation x12, other arithmetic, blocked_factor(): diagonal = lax.linalg.cholesky(rest[:block, :block])  49.8 us
    pallas_call x2, Pallas kernels, group_sum(): pl.pallas_call(lambda *refs: sum_kernel(phases, *refs), out_shape=jax.Sha...  49.2 us
    another operation x8, other arithmetic, blocked_factor(): lax.linalg.triangular_solve(diagonal, eye, left_side=True, lower=True)  42.2 us
    dot_general x41, matrix products, high_dot(): jnp.dot(left, right, precision=lax.Precision.HIGHEST, preferred_element_t...  13.4 us
    dot_general x2, matrix products, apply_kernel(): jnp.einsum('ncj,nij->ci', reach, kernel_tile, precision=lax.Precision.HIG...  9.84 us
  transfers between devices with their start and end apart: 2, of which 0 were waited for; matrix products, arithmetic and copies ran while one was open for 5% of the time, Pallas kernels for 9%

commit v1 on v0

--- a/solution.py
+++ b/solution.py
@@ -405,6 +405,7 @@
 
     sketch_rows = omega.shape[0]
     omega_rows = lax.dynamic_slice_in_dim(omega, samp_idx * (sketch_rows // n_samp), sketch_rows // n_samp)
+    reach_blocks, omega_rows = lax.optimization_barrier((reach_blocks, omega_rows))
     sketch_own = apply_kernel(omega_rows, wide=True) + sketch_shift * omega_rows
     sketch = lax.all_gather(sketch_own, "samp", axis=0, tiled=True)
     rhs = observed[None, :] - prior_draws

time: 338 us -> 327 us (0.967)
  the two profiles are of different devices: /device:TPU:4 before, /device:TPU:8 now
where the time goes in v1:
time: 327 us; the launch traced here: 321 us
  Pallas kernels  155 us (47%)
  other arithmetic  108 us (33%)
  matrix products  27.6 us (8%)
  waiting for transfers between devices  12 us (4%)
  local copies, waits for them, and re-layouts  9.28 us (3%)
  starting transfers between devices  4.41 us (1%)
    pallas_call x4, Pallas kernels, halo_gather(): pl.pallas_call(lambda *refs: halo_kernel(n_blk, n_leaf, wide, *refs), out...  56.6 us
    pallas_call x1, Pallas kernels, gram_sum(): pl.pallas_call(lambda *refs: gram_kernel(phases, *refs), out_shape=(jax.S...  55.5 us
    another operation x12, other arithmetic, blocked_factor(): diagonal = lax.linalg.cholesky(rest[:block, :block])  49.7 us
    pallas_call x2, Pallas kernels, group_sum(): pl.pallas_call(lambda *refs: sum_kernel(phases, *refs), out_shape=jax.Sha...  42.8 us
    another operation x8, other arithmetic, blocked_factor(): lax.linalg.triangular_solve(diagonal, eye, left_side=True, lower=True)  42 us
    dot_general x41, matrix products, high_dot(): jnp.dot(left, right, precision=lax.Precision.HIGHEST, preferred_element_t...  13.5 us
    ppermute x2, waiting for transfers between devices, shifted_2(): return lax.ppermute(block, axis, route)  12 us
    dot_general x2, matrix products, apply_kernel(): jnp.einsum('ncj,nij->ci', reach, kernel_tile, precision=lax.Precision.HIG...  9.84 us
  transfers between devices with their start and end apart: 2, of which 2 were waited for; matrix products, arithmetic and copies ran while one was open for 5% of the time, Pallas kernels for 0%

profile of v1, /device:TPU:8, one launch (start us, length us, event | category | flops | bytes accessed | tf_op | source)
XLA Modules:
  0.0 320.9 jit_solution(8686135028397656638)
XLA Ops:
  0.7 14.9 %shard_map.68 = f32[12,3,256]{2,1,0:T(4,128)} custom-call(f32[3,256]{1,0:T(4,128)} %refs_0_.1), custom_call_target="tpu_custom_call" | custom-call | tf_op jit(solution)/shard_map/pallas_call | solution.py:310
  16.3 15.4 %shard_map.69 = f32[4,256,256]{2,1,0:T(8,128)} custom-call(f32[256,256]{1,0:T(8,128)} %constant_dynamic-slice_fusion.refs_0_), custom_call_target="tpu_custom_call" | custom-call | tf_op jit(solution)/shard_map/pallas_call | solution.py:310
  31.7 4.4 %collective-permute-start.1 = (f32[4,256,256]{2,1,0:T(8,128)}, f32[4,256,256]{2,1,0:T(8,128)S(1)}, u32[]{:S(2)}, u32[]{:S(2)}) collective-permute-start(f32[4,256,256]{2,1,0:T(8,128)} %shard_map.69), channel_id=1, source_target_pairs={{8,0},{16,8},{24,16},{32,24},{40,32},{48,40},{56,48},{64,56},{72,6... | collective-permute-start | bytes 3145736 | tf_op jit(solution)/shard_map/ppermute | solution.py:22
  36.9 5.5 %broadcast_subtract_fusion = f32[12,3,256,256]{3,2,0,1:T(8,128)} fusion(f32[12,3,256]{2,0,1:T(8,128)S(1)} %copy.25, f32[3,256]{1,0:T(4,128)} %refs_0_.1), kind=kLoop, calls=%fused_computation.2 | loop fusion | flops 2359296 | bytes 9477120 | tf_op jit(solution)/shard_map/sub | solution.py:26
  43.1 6.4 %multiply_multiply_fusion = f32[12,256,256]{2,1,0:T(8,128)S(1)} fusion(f32[12,3,256,256]{3,2,0,1:T(8,128)} %broadcast_subtract_fusion, f32[12]{0:T(128)S(1)} %scatter_custom_fusion), kind=kLoop, calls=%fused_computation.15 | loop fusion | flops 17301504 | bytes 12582960 | tf_op jit(solution)/shard_map/mul | solution.py:380
  49.6 1.0 convolution_bitcast_fusion.1
  50.6 7.7 %collective-permute-done.1 = f32[4,256,256]{2,1,0:T(8,128)S(1)} collective-permute-done((f32[4,256,256]{2,1,0:T(8,128)}, f32[4,256,256]{2,1,0:T(8,128)S(1)}, u32[]{:S(2)}, u32[]{:S(2)}) %collective-permute-start.1) | collective-permute-done | bytes 1048608 | tf_op jit(solution)/shard_map/ppermute | solution.py:22
  58.3 1.0 convolution_bitcast_fusion
  59.3 4.4 %collective-permute-done = f32[4,256,256]{2,1,0:T(8,128)S(1)} collective-permute-done((f32[4,256,256]{2,1,0:T(8,128)}, f32[4,256,256]{2,1,0:T(8,128)S(1)}, u32[]{:S(2)}, u32[]{:S(2)}) %collective-permute-start) | collective-permute-done | bytes 1048608 | tf_op jit(solution)/shard_map/ppermute | solution.py:22
  63.7 1.0 fusion.12
  64.8 2.6 all_gather.3
  69.3 0.8 reshape.134.refs_0_
  71.4 55.5 %shard_map.70 = (f32[2048,128]{1,0:T(8,128)}, f32[128,128]{1,0:T(8,128)}) custom-call(f32[1024,128]{1,0:T(8,128)} %reshape.134.refs_0_, f32[128,128]{1,0:T(8,128)} %reshape.135.refs_1_), custom_call_target="tpu_custom_call" | custom-call | tf_op jit(solution)/shard_map/pallas_call | solution.py:240
  128.5 1.4 reshape.136
  130.1 11.7 %custom-call.12 = f32[128,128]{1,0:T(8,128)S(1)} custom-call(f32[128,128]{1,0:T(8,128)S(1)} %fusion.50), custom_call_target="Cholesky" | custom-call | tf_op jit(solution)/shard_map/cholesky/custom-call.1 | solution.py:330
  143.1 9.8 %custom-call.13 = f32[1,128,128]{1,2,0:T(8,128)S(1)} custom-call(f32[1,128,128]{2,1,0:T(8,128)S(1)} %fusion.31), custom_call_target="InvertDiagBlocksLowerTriangular" | custom-call | tf_op jit(solution)/shard_map/triangular_solve/custom-call.0 | solution.py:331
  155.2 11.9 %custom-call.14 = f32[128,128]{1,0:T(8,128)S(1)} custom-call(f32[128,128]{1,0:T(8,128)S(1)} %copy.33), custom_call_target="Cholesky" | custom-call | tf_op jit(solution)/shard_map/cholesky/custom-call.1 | solution.py:330
  168.4 9.8 %custom-call.15 = f32[1,128,128]{1,2,0:T(8,128)S(1)} custom-call(f32[1,128,128]{2,1,0:T(8,128)S(1)} %fusion.32), custom_call_target="InvertDiagBlocksLowerTriangular" | custom-call | tf_op jit(solution)/shard_map/triangular_solve/custom-call.0 | solution.py:331
  180.3 11.7 %custom-call.16 = f32[128,128]{1,0:T(8,128)S(1)} custom-call(f32[128,128]{1,0:T(8,128)S(1)} %fusion.46), custom_call_target="Cholesky" | custom-call | tf_op jit(solution)/shard_map/cholesky/custom-call.1 | solution.py:330
  193.3 10.0 %custom-call.17 = f32[1,128,128]{1,2,0:T(8,128)S(1)} custom-call(f32[1,128,128]{2,1,0:T(8,128)S(1)} %fusion.33), custom_call_target="InvertDiagBlocksLowerTriangular" | custom-call | tf_op jit(solution)/shard_map/triangular_solve/custom-call.0 | solution.py:331
  204.9 11.7 %custom-call.18 = f32[128,128]{1,0:T(8,128)S(1)} custom-call(f32[128,128]{1,0:T(8,128)S(1)} %broadcast_multiply_fusion), custom_call_target="Cholesky" | custom-call | tf_op jit(solution)/shard_map/cholesky/custom-call.1 | solution.py:330
  217.9 9.8 %custom-call.19 = f32[1,128,128]{1,2,0:T(8,128)S(1)} custom-call(f32[1,128,128]{2,1,0:T(8,128)S(1)} %fusion.34), custom_call_target="InvertDiagBlocksLowerTriangular" | custom-call | tf_op jit(solution)/shard_map/triangular_solve/custom-call.0 | solution.py:331
  229.6 1.0 convolution_subtract_fusion.8.refs_0_
  230.6 13.5 %shard_map.71 = f32[12,32,256]{2,1,0:T(8,128)} custom-call(f32[32,256]{1,0:T(8,128)} %convolution_subtract_fusion.8.refs_0_), custom_call_target="tpu_custom_call" | custom-call | tf_op jit(solution)/shard_map/pallas_call | solution.py:310
  244.1 5.0 %multiply_reduce_fusion.3 = (f32[32]{0:T(128)S(1)}, f32[32]{0:T(128)S(1)}, f32[32]{0:T(128)S(1)}, f32[32]{0:T(128)S(1)}, f32[32]{0:T(128)S(1)}, /*index=5*/f32[32,256]{1,0:T(8,128)S(1)}) fusion(f32[32,256]{1,0:T(8,128)S(1)} %copy-done.4, f32[256]{0:T(256)S(1)} %copy-done.8, f32[32,256]{1,0:T(8,128)} %convolution_subtract_fusion.8.refs_0_, ...), kind=kOutput, calls=%fused_computation.122 | convolution fusion | flops 302088032 | bytes 3638912 | tf_op jit(solution)/shard_map/ncj,nij->ci/dot_general | solution.py:394
  250.7 25.7 %shard_map.72 = f32[136,128]{1,0:T(8,128)} custom-call(f32[136,128]{1,0:T(8,128)} %select_maximum_fusion.refs_0_), custom_call_target="tpu_custom_call" | custom-call | tf_op jit(solution)/shard_map/pallas_call | solution.py:109
  276.4 0.8 slice.142
  281.8 0.9 bitcast_divide_fusion.2
  282.7 1.0 fusion.15.refs_0_
  283.6 12.8 %shard_map.73 = f32[12,32,256]{2,1,0:T(8,128)} custom-call(f32[32,256]{1,0:T(8,128)} %fusion.15.refs_0_), custom_call_target="tpu_custom_call" | custom-call | tf_op jit(solution)/shard_map/pallas_call | solution.py:310
  296.4 4.9 %multiply_reduce_fusion.1 = (f32[32]{0:T(128)S(1)}, f32[32,256]{1,0:T(8,128)S(1)}) fusion(f32[32,256]{1,0:T(8,128)} %fusion.15.refs_0_, f32[12,32,256]{2,1,0:T(8,128)} %shard_map.73, f32[12,256,256]{2,1,0:T(8,128)} %copy-done.1), kind=kOutput, calls=%fused_computation.119 | convolution fusion | flops 302014432 | bytes 3604608 | tf_op jit(solution)/shard_map/ncj,nij->ci/dot_general | solution.py:394
  301.9 17.2 %shard_map.74 = f32[8,128]{1,0:T(8,128)} custom-call(f32[8,128]{1,0:T(8,128)} %pad.9.refs_0_), custom_call_target="tpu_custom_call" | custom-call | tf_op jit(solution)/shard_map/pallas_call | solution.py:109
  (116 shorter events, 27.9 us)
Async XLA Ops:
  0.6 14.9 %copy-start = (f32[512,256]{1,0:T(8,128)S(1)}, f32[512,256]{1,0:T(8,128)}, u32[]{:S(2)}) copy-start(f32[512,256]{1,0:T(8,128)} %param.10) | copy-start | bytes 1572868
  31.7 26.6 %collective-permute-start.1 = (f32[4,256,256]{2,1,0:T(8,128)}, f32[4,256,256]{2,1,0:T(8,128)S(1)}, u32[]{:S(2)}, u32[]{:S(2)}) collective-permute-start(f32[4,256,256]{2,1,0:T(8,128)} %shard_map.69), channel_id=1, source_target_pairs={{8,0},{16,8},{24,16},{32,24},{40,32},{48,40},{56,48},{64,56},{72,6... | collective-permute-start | bytes 3145736 | tf_op jit(solution)/shard_map/ppermute | solution.py:22
  36.1 27.6 %collective-permute-start = (f32[4,256,256]{2,1,0:T(8,128)}, f32[4,256,256]{2,1,0:T(8,128)S(1)}, u32[]{:S(2)}, u32[]{:S(2)}) collective-permute-start(f32[4,256,256]{2,1,0:T(8,128)} %shard_map.69), channel_id=1, source_target_pairs={{248,0},{0,8},{8,16},{16,24},{24,32},{32,40},{40,48},{48,56},{56,6... | collective-permute-start | bytes 3145736 | tf_op jit(solution)/shard_map/ppermute | solution.py:22
  36.9 5.5 %copy-start.9 = (s32[1,8]{1,0:T(1,128)S(1)}, s32[1,8]{1,0:T(1,128)}, u32[]{:S(2)}) copy-start(s32[1,8]{1,0:T(1,128)} %param.9) | copy-start | bytes 100
  43.1 6.4 %copy-start.3 = (f32[4,256,256]{2,1,0:T(8,128)S(1)}, f32[4,256,256]{2,1,0:T(8,128)}, u32[]{:S(2)}) copy-start(f32[4,256,256]{2,1,0:T(8,128)} %shard_map.69) | copy-start | bytes 3145732
  49.5 15.2 %copy-start.1 = (f32[12,256,256]{2,1,0:T(8,128)}, f32[12,256,256]{2,1,0:T(8,128)S(1)}, u32[]{:S(2)}) copy-start(f32[12,256,256]{2,1,0:T(8,128)S(1)} %multiply_multiply_fusion) | copy-start | bytes 9437188
  49.5 14.1 %copy-start.2 = (f32[256,256]{1,0:T(8,128)S(1)}, f32[256,256]{1,0:T(8,128)}, u32[]{:S(2)}) copy-start(f32[256,256]{1,0:T(8,128)} %constant_dynamic-slice_fusion.refs_0_) | copy-start | bytes 786436
  67.4 2.8 copy-start.4
  67.4 2.8 copy-start.8
  229.6 48.4 %copy-start.7 = (f32[128,128]{1,0:T(8,128)S(1)}, f32[128,128]{1,0:T(8,128)}, u32[]{:S(2)}) copy-start(f32[128,128]{1,0:T(8,128)} %get-tuple-element.9) | copy-start | bytes 196612
  249.1 33.6 %copy-start.5 = (f32[32,256]{1,0:T(8,128)S(1)}, f32[32,256]{1,0:T(8,128)}, u32[]{:S(2)}) copy-start(f32[32,256]{1,0:T(8,128)} %convolution_subtract_fusion.8.refs_0_) | copy-start | bytes 98308
  283.6 36.1 %copy-start.6 = (f32[32,256]{1,0:T(8,128)S(1)}, f32[32,256]{1,0:T(8,128)}, u32[]{:S(2)}) copy-start(f32[32,256]{1,0:T(8,128)} %fusion.15.refs_0_) | copy-start | bytes 98308
